TPU v7x, 32 devices: a whole 2x2x4 slice. The times are simulated.
32 devices in a mesh: dp: 4 (over y, x), owner: 8 (over z, core).
Axes of the slice: x: 2, y: 2, z: 4, core: 2. Of those that a mesh axis runs over, the one named last changes fastest.
Arguments:
- sample_rows: bfloat16 [49152, 4096], P(('dp', 'owner')), may hold values from -60 to 60
- start_basis: bfloat16 [4096, 128], P(('dp', 'owner')), may hold values from -0.09375 to 0.09375
Outputs:
- projected: bfloat16 [49152, 128], P(('dp', 'owner'))
- basis: float32 [4096, 128], P(('dp', 'owner'))
All inputs are finite; a program needn't handle non-finite values.
Results may differ from a plain program's by a relative error of at most 0.0056.
Values may be sent and summed in bfloat16 or wider, within the bound.
No kernel may reach another device: no remote copies, remote signals or barrier semaphores. Data moves between devices by JAX's collectives and lax.ppermute only.
A program may use at most 64 MiB of HBM per device.

v0:
```python
import math
import jax
import jax.numpy as jnp
from jax import lax
from jax.sharding import PartitionSpec as P

ITERS = 2


def body(sample_rows, start_basis):
    devices_all = lax.axis_size("dp") * lax.axis_size("owner")
    features = sample_rows.shape[1]
    owned_rows = features // devices_all
    full_start = lax.all_gather(start_basis, ("dp", "owner"), axis=0, tiled=True)
    image = jnp.dot(sample_rows, full_start, preferred_element_type=jnp.float32)
    ortho = jnp.zeros((owned_rows, start_basis.shape[1]), jnp.float32)
    for iteration in range(ITERS):
        image_low = image.astype(jnp.bfloat16)
        whole_term = lax.dot_general(
            sample_rows, image_low, (((0,), (0,)), ((), ())), preferred_element_type=jnp.float32
        )
        sketch = lax.psum(whole_term, ("dp", "owner"))
        gram = lax.dot_general(
            sketch,
            sketch,
            (((0,), (0,)), ((), ())),
            precision=lax.Precision.HIGHEST,
            preferred_element_type=jnp.float32,
        )
        lower = jnp.linalg.cholesky(gram)
        ortho = jax.scipy.linalg.solve_triangular(lower, sketch.T, lower=True).T
        current = ortho.astype(jnp.bfloat16)
        image = jnp.dot(sample_rows, current, preferred_element_type=jnp.float32)
    ortho = lax.dynamic_slice_in_dim(
        ortho, lax.axis_index(("dp", "owner")) * owned_rows, owned_rows, 0
    )
    return (image.astype(jnp.bfloat16), ortho * math.sqrt(features))


def solution(mesh):
    return jax.shard_map(
        body,
        mesh=mesh,
        in_specs=(P(("dp", "owner"), None), P(("dp", "owner"), None)),
        out_specs=(P(("dp", "owner"), None), P(("dp", "owner"), None)),
        check_vma=False,
    )
```

profile of v0, /device:TPU:0, one launch (start us, length us, event | category | flops | bytes accessed | tf_op | source)
XLA Modules:
  0.0 446.1 jit_solution(10812391194538860089)
XLA Ops:
  7.2 0.7 all-gather.2.cloned.1.call-update
  7.9 59.6 %all-gather.2.cloned.1.call-done = bf16[4096,128]{1,0:T(8,128)(2,1)} async-done(((bf16[128,128]{1,0:T(8,128)(2,1)}), bf16[4096,128]{1,0:T(8,128)(2,1)}) %all-gather.2.cloned.1.call-update) | async-done | bytes 1048592 | tf_op jit(solution)/shard_map/all_gather | solution.py:14
  67.5 18.1 %convolution_bitcast_fusion.1 = f32[4096,128]{0,1:T(8,128)} fusion(bf16[1536,4096]{1,0:T(8,128)(2,1)} %param.5, bf16[4096,128]{1,0:T(8,128)(2,1)} %all-gather.2.cloned.1.call-done), kind=kOutput, calls=%fused_computation.1 | convolution fusion | flops 3221422080 | bytes 15728640 | tf_op jit(solution)/shard_map/dot_general | solution.py:19
  85.6 0.2 all-reduce.5.cloned.1.call-start
  85.9 133.6 %all-reduce.3.cloned.1.call-done = f32[4096,128]{0,1:T(8,128)} async-done(((f32[4096,128]{0,1:T(8,128)}), f32[4096,128]{0,1:T(8,128)}) %all-reduce.3.cloned.1.call-update) | async-done | bytes 2097168 | tf_op jit(solution)/shard_map/psum | solution.py:22
  219.5 4.2 fusion.13
  223.8 11.7 %cholesky.44 = f32[128,128]{1,0:T(8,128)S(1)} custom-call(f32[128,128]{1,0:T(8,128)S(1)} %fusion.10), custom_call_target="Cholesky" | custom-call | tf_op jit(solution)/shard_map/jit(cholesky)/cholesky | solution.py:30
  235.5 0.6 compare_reduce_fusion.1
  236.2 0.7 fusion.5
  236.8 9.8 %custom-call.6 = f32[1,128,128]{1,2,0:T(8,128)S(1)} custom-call(f32[1,128,128]{2,1,0:T(8,128)S(1)} %fusion.5), custom_call_target="InvertDiagBlocksLowerTriangular" | custom-call | tf_op jit(solution)/shard_map/jit(_solve_triangular)/triangular_solve | solution.py:31
  246.7 1.9 convolution_convert_fusion
  248.6 15.6 %convolution_bitcast_fusion = f32[4096,128]{0,1:T(8,128)} fusion(bf16[1536,4096]{1,0:T(8,128)(2,1)} %param.5, bf16[128,4096]{1,0:T(8,128)(2,1)S(1)} %convolution_convert_fusion), kind=kOutput, calls=%fused_computation | convolution fusion | flops 3221422080 | bytes 15728640 | tf_op jit(solution)/shard_map/dot_general | solution.py:19
  264.2 133.5 %all-reduce.5.cloned.1.call-done = f32[4096,128]{0,1:T(8,128)} async-done(((f32[4096,128]{0,1:T(8,128)}), f32[4096,128]{0,1:T(8,128)}) %all-reduce.5.cloned.1.call-update) | async-done | bytes 2097168 | tf_op jit(solution)/shard_map/psum | solution.py:22
  397.7 4.2 fusion.14
  402.1 11.7 %cholesky.55 = f32[128,128]{1,0:T(8,128)S(1)} custom-call(f32[128,128]{1,0:T(8,128)S(1)} %fusion.8), custom_call_target="Cholesky" | custom-call | tf_op jit(solution)/shard_map/jit(cholesky)/cholesky | solution.py:30
  413.8 0.6 compare_reduce_fusion
  414.4 0.7 fusion.6
  415.1 9.8 %custom-call.7 = f32[1,128,128]{1,2,0:T(8,128)S(1)} custom-call(f32[1,128,128]{2,1,0:T(8,128)S(1)} %fusion.6), custom_call_target="InvertDiagBlocksLowerTriangular" | custom-call | tf_op jit(solution)/shard_map/jit(_solve_triangular)/triangular_solve | solution.py:31
  424.9 1.9 fusion.1
  426.9 1.3 copy-done.2
  428.2 8.8 %fusion = bf16[1536,128]{0,1:T(8,128)(2,1)S(1)} fusion(bf16[1536,4096]{1,0:T(8,128)(2,1)} %param.5, f32[128,4096]{1,0:T(8,128)S(1)} %fusion.1), kind=kOutput, calls=%fused_computation.6 | convolution fusion | flops 1611333632 | bytes 15073280 | tf_op jit(solution)/shard_map/dot_general | solution.py:33
  437.0 0.9 copy.6
  438.0 0.8 multiply_bitcast_fusion
  438.8 0.7 copy.7
  (15 shorter events, 0.4 us)
Async XLA Ops:
  7.2 60.4 %all-gather.2.cloned.1.call-start = ((), (), s32[]{:S(2)}) async-start(), calls=%async_computation | async-start | bytes 1081344 | tf_op jit(solution)/shard_map/all_gather | solution.py:14
  7.9 211.6 %all-reduce.3.cloned.1.call-start = ((), (), s32[]{:S(2)}) async-start(), calls=%async_computation.1 | async-start | bytes 4194304 | tf_op jit(solution)/shard_map/psum | solution.py:22
  85.6 312.1 %all-reduce.5.cloned.1.call-start = ((), (), s32[]{:S(2)}) async-start(), calls=%async_computation.2 | async-start | bytes 4194304 | tf_op jit(solution)/shard_map/psum | solution.py:22
  219.5 27.2 %copy-start.1 = (f32[4096,128]{0,1:T(8,128)S(1)}, f32[4096,128]{0,1:T(8,128)}, u32[]{:S(2)}) copy-start(f32[4096,128]{0,1:T(8,128)} %all-reduce.3.cloned.1.call-done) | copy-start | bytes 6291460
  397.7 27.2 %copy-start = (f32[4096,128]{0,1:T(8,128)S(1)}, f32[4096,128]{0,1:T(8,128)}, u32[]{:S(2)}) copy-start(f32[4096,128]{0,1:T(8,128)} %all-reduce.5.cloned.1.call-done) | copy-start | bytes 6291460
  426.9 1.4 copy-start.2
Sparse Core Ops, SparseCore 0:
  11.0 56.5 all-gather.1
  85.7 133.6 all-reduce.2
  264.4 133.3 all-reduce.4
where the time goes:
time: 446 us
  waiting for transfers between devices  327 us (73%)
  matrix products  54.7 us (12%)
  other arithmetic  46.6 us (10%)
  between operations  13.9 us (3%)
    psum x2, waiting for transfers between devices, body(): sketch = lax.psum(whole_term, ('dp', 'owner'))  267 us
    all_gather x1, waiting for transfers between devices, body(): lax.all_gather(start_basis, ('dp', 'owner'), axis=0, tiled=True)  59.6 us
    dot_general x2, matrix products, body(): lax.dot_general(sample_rows, image_low, (((0,), (0,)), ((), ())), preferr...  33.7 us
    another operation x6, other arithmetic, body(): lower = jnp.linalg.cholesky(gram)  24.8 us
    another operation x4, other arithmetic, body(): ortho = jax.scipy.linalg.solve_triangular(lower, sketch.T, lower=True).T  20.9 us
  transfers between devices with their start and end apart: 3, of which 3 were waited for; matrix products, arithmetic and copies ran while one was open for 0% of the time, Pallas kernels for 0%

commit v1 on v0

--- a/solution.py
+++ b/solution.py
@@ -11,7 +11,31 @@
     devices_all = lax.axis_size("dp") * lax.axis_size("owner")
     features = sample_rows.shape[1]
     owned_rows = features // devices_all
-    full_start = lax.all_gather(start_basis, ("dp", "owner"), axis=0, tiled=True)
+
+    def rest_the_axis_part(m):
+        p_next, arr_out, state_next = (
+            lax.axis_size(("dp", "owner")),
+            lax.axis_index(("dp", "owner")),
+            m.shape[0],
+        )
+        main, high = (m, 1)
+        while high < p_next:
+            main = jnp.concatenate(
+                [
+                    main,
+                    lax.ppermute(
+                        main,
+                        axis_name=("dp", "owner"),
+                        perm=[(j, (j - high) % p_next) for j in range(p_next)],
+                    ),
+                ],
+                0,
+            )
+            high = 2 * high
+        b_now = jnp.roll(main, arr_out * state_next, 0)
+        return b_now
+
+    full_start = rest_the_axis_part(start_basis)
     image = jnp.dot(sample_rows, full_start, preferred_element_type=jnp.float32)
     ortho = jnp.zeros((owned_rows, start_basis.shape[1]), jnp.float32)
     for iteration in range(ITERS):

time: 446 us -> 432 us (0.969)
  waiting for transfers between devices: 327 us -> 301 us
  starting transfers between devices: 0.3 us -> 8.26 us
    all_gather x1 -> x0, waiting for transfers between devices: 59.6 us -> none  [body(): lax.all_gather(start_basis, ('dp', 'owner'), axis=0, tiled=True)]
    ppermute x0 -> x5, waiting for transfers between devices: none -> 31.9 us  [rest_the_axis_part(): lax.ppermute(main, axis_name=('dp', 'owner'), perm=[(j, (j - high) % p_ne...]
    ppermute x0 -> x5, starting transfers between devices: none -> 8 us  [rest_the_axis_part(): lax.ppermute(main, axis_name=('dp', 'owner'), perm=[(j, (j - high) % p_ne...]
  transfers between devices with their start and end apart: 3 -> 7, of which waited for: 3 -> 7; matrix products, arithmetic and copies ran while one was open for 0% -> 1% of each run, Pallas kernels for 0% -> 0%
where the time goes in v1:
time: 432 us
  waiting for transfers between devices  301 us (70%)
  matrix products  52.2 us (12%)
  other arithmetic  48.9 us (11%)
  between operations  14.2 us (3%)
  starting transfers between devices  8.26 us (2%)
  local copies, waits for them, and re-layouts  7.45 us (2%)
    psum x2, waiting for transfers between devices, body(): sketch = lax.psum(whole_term, ('dp', 'owner'))  269 us
    ppermute x5, waiting for transfers between devices, rest_the_axis_part(): lax.ppermute(main, axis_name=('dp', 'owner'), perm=[(j, (j - high) % p_ne...  31.9 us
    dot_general x2, matrix products, body(): lax.dot_general(sample_rows, image_low, (((0,), (0,)), ((), ())), preferr...  31.1 us
    another operation x6, other arithmetic, body(): lower = jnp.linalg.cholesky(gram)  24.8 us
    another operation x4, other arithmetic, body(): ortho = jax.scipy.linalg.solve_triangular(lower, sketch.T, lower=True).T  20.9 us
    dot_general x1, matrix products, body(): image = jnp.dot(sample_rows, current, preferred_element_type=jnp.float32)  8.82 us
  transfers between devices with their start and end apart: 7, of which 7 were waited for; matrix products, arithmetic and copies ran while one was open for 1% of the time, Pallas kernels for 0%

profile of v1, /device:TPU:0, one launch (start us, length us, event | category | flops | bytes accessed | tf_op | source)
XLA Modules:
  0.0 431.7 jit_solution(1256492611274300778)
XLA Ops:
  7.2 6.5 %collective-permute-start = (bf16[128,128]{1,0:T(8,128)(2,1)}, bf16[128,128]{1,0:T(8,128)(2,1)S(1)}, u32[]{:S(2)}, u32[]{:S(2)}) collective-permute-start(bf16[128,128]{1,0:T(8,128)(2,1)} %param.6), channel_id=1, source_target_pairs={{0,31},{1,0},{2,1},{3,2},{4,3},{5,4},{6,5},{7,6},{8,7},{9,8},{10,9... | collective-permute-start | bytes 98312 | tf_op jit(solution)/shard_map/ppermute | solution.py:26
  13.7 1.9 collective-permute-done
  16.9 3.7 collective-permute-done.1
  21.5 1.4 constant_dynamic-update-slice_fusion.4
  22.8 7.5 %collective-permute-done.2 = bf16[512,128]{1,0:T(8,128)(2,1)S(1)} collective-permute-done((bf16[512,128]{1,0:T(8,128)(2,1)S(1)}, bf16[512,128]{1,0:T(8,128)(2,1)S(1)}, u32[]{:S(2)}, u32[]{:S(2)}) %collective-permute-start.2) | collective-permute-done | bytes 131104 | tf_op jit(solution)/shard_map/ppermute | solution.py:26
  33.1 6.4 %collective-permute-done.3 = bf16[1024,128]{1,0:T(8,128)(2,1)S(1)} collective-permute-done((bf16[1024,128]{1,0:T(8,128)(2,1)S(1)}, bf16[1024,128]{1,0:T(8,128)(2,1)S(1)}, u32[]{:S(2)}, u32[]{:S(2)}) %collective-permute-start.3) | collective-permute-done | bytes 262176 | tf_op jit(solution)/shard_map/ppermute | solution.py:26
  40.2 0.9 collective-permute-start.4
  41.1 12.4 %collective-permute-done.4 = bf16[2048,128]{1,0:T(8,128)(2,1)S(1)} collective-permute-done((bf16[2048,128]{1,0:T(8,128)(2,1)}, bf16[2048,128]{1,0:T(8,128)(2,1)S(1)}, u32[]{:S(2)}, u32[]{:S(2)}) %collective-permute-start.4) | collective-permute-done | bytes 524320 | tf_op jit(solution)/shard_map/ppermute | solution.py:26
  53.8 15.5 %convolution_bitcast_fusion.1 = f32[4096,128]{0,1:T(8,128)} fusion(bf16[1536,4096]{1,0:T(8,128)(2,1)} %param.5, bf16[8192,128]{1,0:T(8,128)(2,1)S(1)} %constant_dynamic-update-slice_fusion.5, s32[]{:T(128)S(6)} %select_n.20), kind=kOutput, calls=%fused_computation.1 | convolution fusion | flops 3221422080 | bytes 28311556 | tf_op jit(solution)/shard_map/dot_general | solution.py:43
  69.6 135.2 %all-reduce.3.cloned.1.call-done = f32[4096,128]{0,1:T(8,128)} async-done(((f32[4096,128]{0,1:T(8,128)}), f32[4096,128]{0,1:T(8,128)}) %all-reduce.3.cloned.1.call-update) | async-done | bytes 2097168 | tf_op jit(solution)/shard_map/psum | solution.py:46
  204.8 4.2 fusion.18
  209.1 11.7 %cholesky.44 = f32[128,128]{1,0:T(8,128)S(1)} custom-call(f32[128,128]{1,0:T(8,128)S(1)} %fusion.13), custom_call_target="Cholesky" | custom-call | tf_op jit(solution)/shard_map/jit(cholesky)/cholesky | solution.py:54
  222.2 9.8 %custom-call.6 = f32[1,128,128]{1,2,0:T(8,128)S(1)} custom-call(f32[1,128,128]{2,1,0:T(8,128)S(1)} %fusion.8), custom_call_target="InvertDiagBlocksLowerTriangular" | custom-call | tf_op jit(solution)/shard_map/jit(_solve_triangular)/triangular_solve | solution.py:55
  232.0 1.9 convolution_convert_fusion
  233.9 15.6 %convolution_bitcast_fusion = f32[4096,128]{0,1:T(8,128)} fusion(bf16[1536,4096]{1,0:T(8,128)(2,1)} %param.5, bf16[128,4096]{1,0:T(8,128)(2,1)S(1)} %convolution_convert_fusion), kind=kOutput, calls=%fused_computation | convolution fusion | flops 3221422080 | bytes 15728640 | tf_op jit(solution)/shard_map/dot_general | solution.py:43
  249.6 133.6 %all-reduce.5.cloned.1.call-done = f32[4096,128]{0,1:T(8,128)} async-done(((f32[4096,128]{0,1:T(8,128)}), f32[4096,128]{0,1:T(8,128)}) %all-reduce.5.cloned.1.call-update) | async-done | bytes 2097168 | tf_op jit(solution)/shard_map/psum | solution.py:46
  383.1 4.2 fusion.19
  387.4 11.7 %cholesky.55 = f32[128,128]{1,0:T(8,128)S(1)} custom-call(f32[128,128]{1,0:T(8,128)S(1)} %fusion.11), custom_call_target="Cholesky" | custom-call | tf_op jit(solution)/shard_map/jit(cholesky)/cholesky | solution.py:54
  400.5 9.8 %custom-call.7 = f32[1,128,128]{1,2,0:T(8,128)S(1)} custom-call(f32[1,128,128]{2,1,0:T(8,128)S(1)} %fusion.9), custom_call_target="InvertDiagBlocksLowerTriangular" | custom-call | tf_op jit(solution)/shard_map/jit(_solve_triangular)/triangular_solve | solution.py:55
  410.3 1.9 fusion.1
  412.2 1.3 copy-done.2
  413.6 8.8 %fusion = bf16[1536,128]{0,1:T(8,128)(2,1)S(1)} fusion(bf16[1536,4096]{1,0:T(8,128)(2,1)} %param.5, f32[128,4096]{1,0:T(8,128)S(1)} %fusion.1), kind=kOutput, calls=%fused_computation.6 | convolution fusion | flops 1611333632 | bytes 15073280 | tf_op jit(solution)/shard_map/dot_general | solution.py:57
  422.4 0.9 copy.6
  423.3 0.8 multiply_bitcast_fusion
  (39 shorter events, 9.8 us)
Async XLA Ops:
  7.2 46.5 %copy-start.3 = (bf16[128,128]{1,0:T(8,128)(2,1)S(1)}, bf16[128,128]{1,0:T(8,128)(2,1)}, u32[]{:S(2)}) copy-start(bf16[128,128]{1,0:T(8,128)(2,1)} %param.6) | copy-start | bytes 98308
  7.2 197.6 %all-reduce.3.cloned.1.call-start = ((), (), s32[]{:S(2)}) async-start(), calls=%async_computation | async-start | bytes 4194304 | tf_op jit(solution)/shard_map/psum | solution.py:46
  7.2 8.4 %collective-permute-start = (bf16[128,128]{1,0:T(8,128)(2,1)}, bf16[128,128]{1,0:T(8,128)(2,1)S(1)}, u32[]{:S(2)}, u32[]{:S(2)}) collective-permute-start(bf16[128,128]{1,0:T(8,128)(2,1)} %param.6), channel_id=1, source_target_pairs={{0,31},{1,0},{2,1},{3,2},{4,3},{5,4},{6,5},{7,6},{8,7},{9,8},{10,9... | collective-permute-start | bytes 98312 | tf_op jit(solution)/shard_map/ppermute | solution.py:26
  16.4 4.3 collective-permute-start.1
  21.4 9.0 %collective-permute-start.2 = (bf16[512,128]{1,0:T(8,128)(2,1)S(1)}, bf16[512,128]{1,0:T(8,128)(2,1)S(1)}, u32[]{:S(2)}, u32[]{:S(2)}) collective-permute-start(bf16[512,128]{1,0:T(8,128)(2,1)S(1)} %pad_maximum_fusion.1), channel_id=1, source_target_pairs={{0,28},{1,29},{2,30},{3,31},{4,0},{5,1},{6,2},{7,3},{8,4},{9,5},{1... | collective-permute-start | bytes 393224 | tf_op jit(solution)/shard_map/ppermute | solution.py:26
  31.1 8.4 %collective-permute-start.3 = (bf16[1024,128]{1,0:T(8,128)(2,1)S(1)}, bf16[1024,128]{1,0:T(8,128)(2,1)S(1)}, u32[]{:S(2)}, u32[]{:S(2)}) collective-permute-start(bf16[1024,128]{1,0:T(8,128)(2,1)S(1)} %pad_maximum_fusion), channel_id=1, source_target_pairs={{0,24},{1,25},{2,26},{3,27},{4,28},{5,29},{6,30},{7,31},{8,0},{9,1... | collective-permute-start | bytes 786440 | tf_op jit(solution)/shard_map/ppermute | solution.py:26
  40.2 13.3 %collective-permute-start.4 = (bf16[2048,128]{1,0:T(8,128)(2,1)}, bf16[2048,128]{1,0:T(8,128)(2,1)S(1)}, u32[]{:S(2)}, u32[]{:S(2)}) collective-permute-start(bf16[2048,128]{1,0:T(8,128)(2,1)} %get-tuple-element.6), channel_id=1, source_target_pairs={{0,16},{1,17},{2,18},{3,19},{4,20},{5,21},{6,22},{7,23},{8,24},{9,... | collective-permute-start | bytes 1572872 | tf_op jit(solution)/shard_map/ppermute | solution.py:26
  69.3 313.8 %all-reduce.5.cloned.1.call-start = ((), (), s32[]{:S(2)}) async-start(), calls=%async_computation.1 | async-start | bytes 4194304 | tf_op jit(solution)/shard_map/psum | solution.py:46
  204.8 27.2 %copy-start.1 = (f32[4096,128]{0,1:T(8,128)S(1)}, f32[4096,128]{0,1:T(8,128)}, u32[]{:S(2)}) copy-start(f32[4096,128]{0,1:T(8,128)} %all-reduce.3.cloned.1.call-done) | copy-start | bytes 6291460
  383.1 27.2 %copy-start = (f32[4096,128]{0,1:T(8,128)S(1)}, f32[4096,128]{0,1:T(8,128)}, u32[]{:S(2)}) copy-start(f32[4096,128]{0,1:T(8,128)} %all-reduce.5.cloned.1.call-done) | copy-start | bytes 6291460
  412.2 1.3 copy-start.2
Sparse Core Ops, SparseCore 0:
  69.4 135.2 all-reduce.2
  249.7 133.3 all-reduce.4
